TPU v7x, 32 devices: a whole 2x2x4 slice. The times are simulated.
32 devices in a mesh: chain: 8 (over z, y), col: 4 (over x, core).
Axes of the slice: x: 2, y: 2, z: 4, core: 2. Of those that a mesh axis runs over, the one named last changes fastest.
Arguments:
- rhs: bfloat16 [4, 8, 32, 128], P(None, 'chain'), may hold values from -6 to 6
- pattern: int32 [4, 8, 24], P(None, 'chain', 'col'), may hold values from 0 to 31, as said below
- factor: bfloat16 [4, 8, 24, 128, 128], P(None, 'chain', 'col'), may hold values from -0.1875 to 0.1875
- inverse: bfloat16 [4, 8, 128, 128], P(None, 'chain'), as said below
- level_size: int32 [6], replicated, may hold values from 1 to 8, 32 in all
Outputs:
- half_solved: bfloat16 [4, 8, 32, 128], P(None, 'chain')
- solved: bfloat16 [4, 8, 32, 128], P(None, 'chain')
Inputs may be any that keep to these rules, and one draw needn't show every extreme that they name: Among the pattern entries held by one index of chain and one index of col (all 4 of its block rows), at most 3 name block rows on any one index of chain (block row mod 8); in every such group exactly 3 name block rows on one index of chain that is common to all groups of that index of col. A block row may name a block row more than once. `inverse`: each block is lower triangular with a diagonal between 0.3 and 2.
All inputs are finite; a program needn't handle non-finite values.
Results may differ from a plain program's by a relative error of at most 0.013.
Values may be sent and summed in bfloat16 or wider, within the bound.
A program may use at most 64 MiB of HBM per device.

v0:
```python
import jax
import jax.numpy as jnp
from jax import lax
from jax.sharding import PartitionSpec as P


def level_index(positions, ends):
    return jnp.sum((positions[..., None] >= ends).astype(jnp.int32), axis=-1)


def per_device(rhs, pattern, factor, inverse, level_size):
    lane_count = lax.axis_size("chain")
    chain_pos = lax.axis_index("chain")
    row_count = rhs.shape[0]
    probe_count = rhs.shape[2]
    width = rhs.shape[3]
    entries = pattern.shape[2]
    level_count = level_size.shape[0]
    total = row_count * lane_count
    ends = jnp.cumsum(level_size)
    starts = ends - level_size
    own_rows = jnp.arange(row_count, dtype=jnp.int32) * lane_count + chain_pos
    own_level = level_index(own_rows, ends)
    columns = pattern[:, 0, :]
    column_level = level_index(columns, ends)
    keep = column_level < own_level[:, None]
    blocks = factor[:, 0]
    inverse_rows = inverse[:, 0]
    right = rhs[:, 0]
    slot_ids = jnp.arange(row_count, dtype=jnp.int32)
    lane_ids = jnp.arange(lane_count, dtype=jnp.int32)

    def locate(level):
        picked = own_level == level
        own_slot = jnp.sum(jnp.where(picked, slot_ids, 0))
        return (picked, own_slot, jnp.any(picked))

    def forward_level(level, carry):
        store, half_local = carry
        picked, own_slot, is_live = locate(level)
        wanted = keep[own_slot] & is_live
        chosen = jnp.where(
            wanted[:, None, None], store[columns[own_slot]], jnp.zeros((), jnp.bfloat16)
        )
        partial_value = jnp.einsum(
            "jpb,jcb->pc", chosen, blocks[own_slot], preferred_element_type=jnp.float32
        )
        summed = lax.psum(partial_value, "col")
        rest = (right[own_slot].astype(jnp.float32) - summed).astype(jnp.bfloat16)
        segment = jnp.dot(
            rest, inverse_rows[own_slot].T, preferred_element_type=jnp.float32
        ).astype(jnp.bfloat16)
        segment = jnp.where(is_live, segment, jnp.zeros((), jnp.bfloat16))
        front = lax.all_gather(segment[None], "chain", axis=0, tiled=True)
        half_local = jnp.where(picked[:, None, None], segment[None], half_local)
        start = starts[level]
        ordered = front[(start + lane_ids) % lane_count]
        store = lax.dynamic_update_slice_in_dim(store, ordered, start, 0)
        return (store, half_local)

    store = jnp.zeros((total + lane_count, probe_count, width), jnp.bfloat16)
    half_local = jnp.zeros((row_count, probe_count, width), jnp.bfloat16)
    store, half_local = lax.fori_loop(0, level_count, forward_level, (store, half_local))
    solved_local = jnp.zeros((row_count, probe_count, width), jnp.bfloat16)
    count = row_count * entries
    capacity = max(2, (count + lane_count - 1) // lane_count)
    slots_all = lane_count * capacity
    flat_cols = columns.reshape(count)
    flat_src = jnp.broadcast_to(own_rows[:, None], (row_count, entries)).reshape(count)
    dest = flat_cols % lane_count
    onehot = (dest[:, None] == lane_ids[None, :]).astype(jnp.int32)
    before = jnp.cumsum(onehot, axis=0) - onehot
    rank = jnp.sum(before * onehot, axis=1)
    slot = dest * capacity + rank
    select = slot[None, :] == jnp.arange(slots_all, dtype=jnp.int32)[:, None]
    sent_blocks = jnp.dot(
        select.astype(jnp.bfloat16),
        blocks.reshape(count, width * width),
        preferred_element_type=jnp.float32,
    )
    sent_blocks = sent_blocks.astype(jnp.bfloat16).reshape(lane_count, capacity, width, width)
    sent_src = jnp.sum(jnp.where(select, flat_src[None, :] + 1, 0), axis=1) - 1
    sent_dst = jnp.sum(jnp.where(select, flat_cols[None, :] + 1, 0), axis=1) - 1
    sent_meta = jnp.stack([sent_src, sent_dst], axis=1).reshape(lane_count, capacity, 2)
    home_blocks, home_meta = (
        lax.all_to_all(sent_blocks, "chain", split_axis=0, concat_axis=0, tiled=True),
        lax.all_to_all(sent_meta, "chain", split_axis=0, concat_axis=0, tiled=True),
    )
    home_blocks = home_blocks.reshape(slots_all, width, width)
    home_meta = home_meta.reshape(slots_all, 2)
    source_row = home_meta[:, 0]
    target_row = home_meta[:, 1]
    valid = source_row >= 0
    source_level = level_index(source_row, ends)
    target_level = level_index(target_row, ends)
    home_keep = valid & (target_level < source_level)
    source_lane = jnp.where(valid, source_row % lane_count, 0)
    home_slot = jnp.where(valid, target_row // lane_count, -1)

    def home_level(counter, carry):
        accum, solved_now = carry
        level = level_count - 1 - counter
        picked, own_slot, is_live = locate(level)
        summed = lax.psum(accum[own_slot], "col")
        rest = (half_local[own_slot].astype(jnp.float32) - summed).astype(jnp.bfloat16)
        segment = jnp.dot(rest, inverse_rows[own_slot], preferred_element_type=jnp.float32).astype(
            jnp.bfloat16
        )
        segment = jnp.where(is_live, segment, jnp.zeros((), jnp.bfloat16))
        solved_now = jnp.where(picked[:, None, None], segment[None], solved_now)
        front = lax.all_gather(segment[None], "chain", axis=0, tiled=True)
        active = home_keep & (source_level == level)
        incoming = front[source_lane]
        terms = jnp.einsum(
            "kpc,kcb->kpb", incoming, home_blocks, preferred_element_type=jnp.float32
        )
        spread = ((home_slot[None, :] == slot_ids[:, None]) & active[None, :]).astype(jnp.float32)
        added = jnp.dot(
            spread,
            terms.reshape(slots_all, probe_count * width),
            precision=lax.Precision.HIGHEST,
            preferred_element_type=jnp.float32,
        )
        accum = accum + added.reshape(row_count, probe_count, width)
        return (accum, solved_now)

    accum = jnp.zeros((row_count, probe_count, width), jnp.float32)
    accum, solved_local = lax.fori_loop(0, level_count, home_level, (accum, solved_local))
    return (half_local[:, None], solved_local[:, None])


def solution(mesh):
    return jax.shard_map(
        per_device,
        mesh=mesh,
        in_specs=(
            P(None, "chain", None, None),
            P(None, "chain", "col"),
            P(None, "chain", "col", None, None),
            P(None, "chain", None, None),
            P(),
        ),
        out_specs=(P(None, "chain", None, None), P(None, "chain", None, None)),
        check_vma=False,
    )
```

profile of v0, /device:TPU:0, one launch (start us, length us, event | category | flops | bytes accessed | tf_op | source)
XLA Modules:
  0.0 617.3 jit_solution(10101479652952594900)
XLA Ops:
  1.1 1.3 reduce.3
  4.0 7.3 %all-to-all-start = ((s32[8,3,2]{1,2,0:T(2,128)}), s32[8,3,2]{1,2,0:T(2,128)S(1)}, u32[]{:S(2)}, u32[]{:S(2)}) async-start(s32[8,3,2]{1,2,0:T(2,128)} %copy.16), calls=%async_computation | async-start | bytes 16384 | tf_op jit(solution)/shard_map/all_to_all | solution.py:87
  11.3 0.8 reduce-window.8
  14.0 1.8 fusion.43
  15.9 1.0 copy.21
  17.0 0.9 all-to-all-done
  17.8 5.3 all-to-all-start.1
  23.2 314.8 %while.35 = (s32[]{:T(128)}, bf16[40,32,128]{2,1,0:T(8,128)(2,1)S(1)}, bf16[4,32,128]{2,1,0:T(8,128)(2,1)S(1)}, s32[4]{0:T(128)S(1)}, bf16[4,32,128]{2,1,0:T(8,1...) while((s32[]{:T(128)}, ...), condition=%wide.region_7.8_spmd.clone, body=%wide.region_3.7_spmd.clone.sunk | while | flops 7424167 | bytes 878571 | solution.py:63
  28.3 1.1 convolution_bitcast_fusion.2
  29.5 10.4 %psum.30 = f32[32,128]{1,0:T(8,128)S(1)} all-reduce(f32[32,128]{1,0:T(8,128)S(1)} %convolution_bitcast_fusion.2), channel_id=1, replica_groups=mesh['chain'=8,'col'=4] {'col'}, use_global_device_ids=true, to_apply=%region_6.6 | all-reduce | flops 4096 | bytes 32768 | tf_op jit(solution)/shard_map/while/body/eval_jaxpr/psum | solution.py:48
  39.9 1.5 fusion.84
  41.4 31.1 %all-gather.6 = bf16[256,128]{1,0:T(8,128)(2,1)S(1)} all-gather(bf16[32,128]{1,0:T(8,128)(2,1)S(1)} %fusion.84), channel_id=2, replica_groups=mesh['chain'=8,'col'=4] {'chain'}, dimensions={0}, use_global_device_ids=true | all-gather | bytes 73728 | tf_op jit(solution)/shard_map/while/body/eval_jaxpr/all_gather | solution.py:54
  81.5 1.1 convolution_bitcast_fusion.2
  82.6 10.1 %psum.30 = f32[32,128]{1,0:T(8,128)S(1)} all-reduce(f32[32,128]{1,0:T(8,128)S(1)} %convolution_bitcast_fusion.2), channel_id=1, replica_groups=mesh['chain'=8,'col'=4] {'col'}, use_global_device_ids=true, to_apply=%region_6.6 | all-reduce | flops 4096 | bytes 32768 | tf_op jit(solution)/shard_map/while/body/eval_jaxpr/psum | solution.py:48
  92.8 1.5 fusion.84
  94.2 30.6 %all-gather.6 = bf16[256,128]{1,0:T(8,128)(2,1)S(1)} all-gather(bf16[32,128]{1,0:T(8,128)(2,1)S(1)} %fusion.84), channel_id=2, replica_groups=mesh['chain'=8,'col'=4] {'chain'}, dimensions={0}, use_global_device_ids=true | all-gather | bytes 73728 | tf_op jit(solution)/shard_map/while/body/eval_jaxpr/all_gather | solution.py:54
  133.8 1.1 convolution_bitcast_fusion.2
  135.0 10.1 %psum.30 = f32[32,128]{1,0:T(8,128)S(1)} all-reduce(f32[32,128]{1,0:T(8,128)S(1)} %convolution_bitcast_fusion.2), channel_id=1, replica_groups=mesh['chain'=8,'col'=4] {'col'}, use_global_device_ids=true, to_apply=%region_6.6 | all-reduce | flops 4096 | bytes 32768 | tf_op jit(solution)/shard_map/while/body/eval_jaxpr/psum | solution.py:48
  145.1 1.5 fusion.84
  146.6 30.6 %all-gather.6 = bf16[256,128]{1,0:T(8,128)(2,1)S(1)} all-gather(bf16[32,128]{1,0:T(8,128)(2,1)S(1)} %fusion.84), channel_id=2, replica_groups=mesh['chain'=8,'col'=4] {'chain'}, dimensions={0}, use_global_device_ids=true | all-gather | bytes 73728 | tf_op jit(solution)/shard_map/while/body/eval_jaxpr/all_gather | solution.py:54
  186.2 1.1 convolution_bitcast_fusion.2
  187.3 10.1 %psum.30 = f32[32,128]{1,0:T(8,128)S(1)} all-reduce(f32[32,128]{1,0:T(8,128)S(1)} %convolution_bitcast_fusion.2), channel_id=1, replica_groups=mesh['chain'=8,'col'=4] {'col'}, use_global_device_ids=true, to_apply=%region_6.6 | all-reduce | flops 4096 | bytes 32768 | tf_op jit(solution)/shard_map/while/body/eval_jaxpr/psum | solution.py:48
  197.4 1.5 fusion.84
  198.9 30.6 %all-gather.6 = bf16[256,128]{1,0:T(8,128)(2,1)S(1)} all-gather(bf16[32,128]{1,0:T(8,128)(2,1)S(1)} %fusion.84), channel_id=2, replica_groups=mesh['chain'=8,'col'=4] {'chain'}, dimensions={0}, use_global_device_ids=true | all-gather | bytes 73728 | tf_op jit(solution)/shard_map/while/body/eval_jaxpr/all_gather | solution.py:54
  238.5 1.1 convolution_bitcast_fusion.2
  239.6 10.1 %psum.30 = f32[32,128]{1,0:T(8,128)S(1)} all-reduce(f32[32,128]{1,0:T(8,128)S(1)} %convolution_bitcast_fusion.2), channel_id=1, replica_groups=mesh['chain'=8,'col'=4] {'col'}, use_global_device_ids=true, to_apply=%region_6.6 | all-reduce | flops 4096 | bytes 32768 | tf_op jit(solution)/shard_map/while/body/eval_jaxpr/psum | solution.py:48
  249.8 1.5 fusion.84
  251.2 30.6 %all-gather.6 = bf16[256,128]{1,0:T(8,128)(2,1)S(1)} all-gather(bf16[32,128]{1,0:T(8,128)(2,1)S(1)} %fusion.84), channel_id=2, replica_groups=mesh['chain'=8,'col'=4] {'chain'}, dimensions={0}, use_global_device_ids=true | all-gather | bytes 73728 | tf_op jit(solution)/shard_map/while/body/eval_jaxpr/all_gather | solution.py:54
  290.8 1.1 convolution_bitcast_fusion.2
  291.9 10.1 %psum.30 = f32[32,128]{1,0:T(8,128)S(1)} all-reduce(f32[32,128]{1,0:T(8,128)S(1)} %convolution_bitcast_fusion.2), channel_id=1, replica_groups=mesh['chain'=8,'col'=4] {'col'}, use_global_device_ids=true, to_apply=%region_6.6 | all-reduce | flops 4096 | bytes 32768 | tf_op jit(solution)/shard_map/while/body/eval_jaxpr/psum | solution.py:48
  302.1 1.5 fusion.84
  303.6 30.6 %all-gather.6 = bf16[256,128]{1,0:T(8,128)(2,1)S(1)} all-gather(bf16[32,128]{1,0:T(8,128)(2,1)S(1)} %fusion.84), channel_id=2, replica_groups=mesh['chain'=8,'col'=4] {'chain'}, dimensions={0}, use_global_device_ids=true | all-gather | bytes 73728 | tf_op jit(solution)/shard_map/while/body/eval_jaxpr/all_gather | solution.py:54
  338.2 278.4 %while.36 = (s32[]{:T(128)}, f32[4,32,128]{2,0,1:T(4,128)S(1)}, bf16[4,32,128]{2,1,0:T(8,128)(2,1)S(1)}, s32[24]{0:T(128)S(1)}, s32[24]{0:T(128)S(1)}, /*index=5...) while((s32[]{:T(128)}, f32[4,32,128]{2,0,1:T(4,128)S(1)}, ...), condition=%wide.region_18.19_spmd.clone.clone, body=%wide.region_14.18_spmd.clone.clone.sunk | while | flops 31024460 | bytes 2709372 | solution.py:128
  341.7 10.1 %psum.31 = f32[32,128]{1,0:T(8,128)S(1)} all-reduce(f32[32,128]{1,0:T(8,128)S(1)} %bitcast.150), channel_id=1, replica_groups=mesh['chain'=8,'col'=4] {'col'}, use_global_device_ids=true, to_apply=%region_17.17 | all-reduce | flops 4096 | bytes 32768 | tf_op jit(solution)/shard_map/while/body/eval_jaxpr/psum | solution.py:104
  351.8 0.8 fusion.94
  352.6 30.5 %all-gather.7 = bf16[256,128]{1,0:T(8,128)(2,1)S(1)} all-gather(bf16[32,128]{1,0:T(8,128)(2,1)S(1)} %fusion.94), channel_id=3, replica_groups=mesh['chain'=8,'col'=4] {'chain'}, dimensions={0}, use_global_device_ids=true | all-gather | bytes 73728 | tf_op jit(solution)/shard_map/while/body/eval_jaxpr/all_gather | solution.py:111
  388.1 10.1 %psum.31 = f32[32,128]{1,0:T(8,128)S(1)} all-reduce(f32[32,128]{1,0:T(8,128)S(1)} %bitcast.150), channel_id=1, replica_groups=mesh['chain'=8,'col'=4] {'col'}, use_global_device_ids=true, to_apply=%region_17.17 | all-reduce | flops 4096 | bytes 32768 | tf_op jit(solution)/shard_map/while/body/eval_jaxpr/psum | solution.py:104
  399.0 30.5 %all-gather.7 = bf16[256,128]{1,0:T(8,128)(2,1)S(1)} all-gather(bf16[32,128]{1,0:T(8,128)(2,1)S(1)} %fusion.94), channel_id=3, replica_groups=mesh['chain'=8,'col'=4] {'chain'}, dimensions={0}, use_global_device_ids=true | all-gather | bytes 73728 | tf_op jit(solution)/shard_map/while/body/eval_jaxpr/all_gather | solution.py:111
  434.5 10.1 %psum.31 = f32[32,128]{1,0:T(8,128)S(1)} all-reduce(f32[32,128]{1,0:T(8,128)S(1)} %bitcast.150), channel_id=1, replica_groups=mesh['chain'=8,'col'=4] {'col'}, use_global_device_ids=true, to_apply=%region_17.17 | all-reduce | flops 4096 | bytes 32768 | tf_op jit(solution)/shard_map/while/body/eval_jaxpr/psum | solution.py:104
  444.6 0.8 fusion.94
  445.4 30.5 %all-gather.7 = bf16[256,128]{1,0:T(8,128)(2,1)S(1)} all-gather(bf16[32,128]{1,0:T(8,128)(2,1)S(1)} %fusion.94), channel_id=3, replica_groups=mesh['chain'=8,'col'=4] {'chain'}, dimensions={0}, use_global_device_ids=true | all-gather | bytes 73728 | tf_op jit(solution)/shard_map/while/body/eval_jaxpr/all_gather | solution.py:111
  480.9 10.1 %psum.31 = f32[32,128]{1,0:T(8,128)S(1)} all-reduce(f32[32,128]{1,0:T(8,128)S(1)} %bitcast.150), channel_id=1, replica_groups=mesh['chain'=8,'col'=4] {'col'}, use_global_device_ids=true, to_apply=%region_17.17 | all-reduce | flops 4096 | bytes 32768 | tf_op jit(solution)/shard_map/while/body/eval_jaxpr/psum | solution.py:104
  491.0 0.8 fusion.94
  491.8 30.5 %all-gather.7 = bf16[256,128]{1,0:T(8,128)(2,1)S(1)} all-gather(bf16[32,128]{1,0:T(8,128)(2,1)S(1)} %fusion.94), channel_id=3, replica_groups=mesh['chain'=8,'col'=4] {'chain'}, dimensions={0}, use_global_device_ids=true | all-gather | bytes 73728 | tf_op jit(solution)/shard_map/while/body/eval_jaxpr/all_gather | solution.py:111
  527.3 10.1 %psum.31 = f32[32,128]{1,0:T(8,128)S(1)} all-reduce(f32[32,128]{1,0:T(8,128)S(1)} %bitcast.150), channel_id=1, replica_groups=mesh['chain'=8,'col'=4] {'col'}, use_global_device_ids=true, to_apply=%region_17.17 | all-reduce | flops 4096 | bytes 32768 | tf_op jit(solution)/shard_map/while/body/eval_jaxpr/psum | solution.py:104
  538.2 30.5 %all-gather.7 = bf16[256,128]{1,0:T(8,128)(2,1)S(1)} all-gather(bf16[32,128]{1,0:T(8,128)(2,1)S(1)} %fusion.94), channel_id=3, replica_groups=mesh['chain'=8,'col'=4] {'chain'}, dimensions={0}, use_global_device_ids=true | all-gather | bytes 73728 | tf_op jit(solution)/shard_map/while/body/eval_jaxpr/all_gather | solution.py:111
  573.7 10.1 %psum.31 = f32[32,128]{1,0:T(8,128)S(1)} all-reduce(f32[32,128]{1,0:T(8,128)S(1)} %bitcast.150), channel_id=1, replica_groups=mesh['chain'=8,'col'=4] {'col'}, use_global_device_ids=true, to_apply=%region_17.17 | all-reduce | flops 4096 | bytes 32768 | tf_op jit(solution)/shard_map/while/body/eval_jaxpr/psum | solution.py:104
  584.6 30.5 %all-gather.7 = bf16[256,128]{1,0:T(8,128)(2,1)S(1)} all-gather(bf16[32,128]{1,0:T(8,128)(2,1)S(1)} %fusion.94), channel_id=3, replica_groups=mesh['chain'=8,'col'=4] {'chain'}, dimensions={0}, use_global_device_ids=true | all-gather | bytes 73728 | tf_op jit(solution)/shard_map/while/body/eval_jaxpr/all_gather | solution.py:111
  (181 shorter events, 55.2 us)
Async XLA Ops:
  4.0 13.8 %all-to-all-start = ((s32[8,3,2]{1,2,0:T(2,128)}), s32[8,3,2]{1,2,0:T(2,128)S(1)}, u32[]{:S(2)}, u32[]{:S(2)}) async-start(s32[8,3,2]{1,2,0:T(2,128)} %copy.16), calls=%async_computation | async-start | bytes 16384 | tf_op jit(solution)/shard_map/all_to_all | solution.py:87
  17.8 5.3 copy-start.2
  17.8 320.4 %all-to-all-start.1 = ((bf16[8,3,128,128]{3,2,1,0:T(8,128)(2,1)}), bf16[8,3,128,128]{3,2,1,0:T(8,128)(2,1)S(1)}, u32[]{:S(2)}, u32[]{:S(2)}) async-start(bf16[8,3,128,128]{3,2,1,0:T(8,128)(2,1)} %bitcast.42), calls=%async_computation.1 | async-start | bytes 1572864 | tf_op jit(solution)/shard_map/all_to_all | solution.py:86
  616.6 0.6 copy-start
  616.6 0.6 copy-start.1
where the time goes:
time: 619 us; the launch traced here: 617 us
  blocking collectives  489 us (79%)
  loops' own time  36 us (6%)
  other arithmetic  33.2 us (5%)
  matrix products  26.7 us (4%)
  local copies, waits for them, and re-layouts  18.2 us (3%)
  starting transfers between devices  12.6 us (2%)
    all_gather x6, blocking collectives, forward_level(): front = lax.all_gather(segment[None], 'chain', axis=0, tiled=True)  184 us
    all_gather x6, blocking collectives, home_level(): front = lax.all_gather(segment[None], 'chain', axis=0, tiled=True)  183 us
    psum x6, blocking collectives, forward_level(): summed = lax.psum(partial_value, 'col')  61.1 us
    psum x6, blocking collectives, home_level(): summed = lax.psum(accum[own_slot], 'col')  60.7 us
    another operation x1, loops' own time, per_device(): lax.fori_loop(0, level_count, forward_level, (store, half_local))  23.3 us
    another operation x1, loops' own time, per_device(): lax.fori_loop(0, level_count, home_level, (accum, solved_local))  12.7 us
  transfers between devices with their start and end apart: 2, of which 1 were waited for; matrix products, arithmetic and copies ran while one was open for 8% of the time, Pallas kernels for 0%

commit v1 on v0

--- a/solution.py
+++ b/solution.py
@@ -101,7 +101,7 @@
         accum, solved_now = carry
         level = level_count - 1 - counter
         picked, own_slot, is_live = locate(level)
-        summed = lax.psum(accum[own_slot], "col")
+        summed = jnp.sum(lax.all_gather(accum[own_slot], "col"), axis=0)
         rest = (half_local[own_slot].astype(jnp.float32) - summed).astype(jnp.bfloat16)
         segment = jnp.dot(rest, inverse_rows[own_slot], preferred_element_type=jnp.float32).astype(
             jnp.bfloat16

time: 619 us -> 590 us (0.953)
  blocking collectives: 489 us -> 460 us
    psum x6 -> x0, blocking collectives: 60.7 us -> none  [home_level(): summed = lax.psum(accum[own_slot], 'col')]
    all_gather x0 -> x6, blocking collectives: none -> 31.4 us  [home_level(): summed = jnp.sum(lax.all_gather(accum[own_slot], 'col'), axis=0)]
  transfers between devices with their start and end apart: 2 -> 2, of which waited for: 1 -> 1; matrix products, arithmetic and copies ran while one was open for 8% -> 9% of each run, Pallas kernels for 0% -> 0%
where the time goes in v1:
time: 590 us; the launch traced here: 588 us
  blocking collectives  460 us (78%)
  loops' own time  36 us (6%)
  other arithmetic  33.3 us (6%)
  matrix products  26.7 us (5%)
  local copies, waits for them, and re-layouts  18.2 us (3%)
  starting transfers between devices  12.6 us (2%)
    all_gather x6, blocking collectives, forward_level(): front = lax.all_gather(segment[None], 'chain', axis=0, tiled=True)  184 us
    all_gather x6, blocking collectives, home_level(): front = lax.all_gather(segment[None], 'chain', axis=0, tiled=True)  183 us
    psum x6, blocking collectives, forward_level(): summed = lax.psum(partial_value, 'col')  61.1 us
    all_gather x6, blocking collectives, home_level(): summed = jnp.sum(lax.all_gather(accum[own_slot], 'col'), axis=0)  31.4 us
    another operation x1, loops' own time, per_device(): lax.fori_loop(0, level_count, forward_level, (store, half_local))  23.3 us
    another operation x1, loops' own time, per_device(): lax.fori_loop(0, level_count, home_level, (accum, solved_local))  12.7 us
  transfers between devices with their start and end apart: 2, of which 1 were waited for; matrix products, arithmetic and copies ran while one was open for 9% of the time, Pallas kernels for 0%

profile of v1, /device:TPU:0, one launch (start us, length us, event | category | flops | bytes accessed | tf_op | source)
XLA Modules:
  0.0 588.0 jit_solution(14926145971442606721)
XLA Ops:
  1.1 1.3 reduce.3
  4.0 7.3 %all-to-all-start = ((s32[8,3,2]{1,2,0:T(2,128)}), s32[8,3,2]{1,2,0:T(2,128)S(1)}, u32[]{:S(2)}, u32[]{:S(2)}) async-start(s32[8,3,2]{1,2,0:T(2,128)} %copy.18), calls=%async_computation | async-start | bytes 16384 | tf_op jit(solution)/shard_map/all_to_all | solution.py:87
  11.3 0.8 reduce-window.8
  14.0 1.8 fusion.43
  15.9 1.0 copy.23
  17.0 0.9 all-to-all-done
  17.8 5.3 all-to-all-start.1
  23.2 314.8 %while.35 = (s32[]{:T(128)}, bf16[40,32,128]{2,1,0:T(8,128)(2,1)S(1)}, bf16[4,32,128]{2,1,0:T(8,128)(2,1)S(1)}, s32[4]{0:T(128)S(1)}, bf16[4,32,128]{2,1,0:T(8,1...) while((s32[]{:T(128)}, ...), condition=%wide.region_7.8_spmd.clone, body=%wide.region_3.7_spmd.clone.sunk | while | flops 7424167 | bytes 878571 | solution.py:63
  28.3 1.1 convolution_bitcast_fusion.2
  29.5 10.4 %psum.16 = f32[32,128]{1,0:T(8,128)S(1)} all-reduce(f32[32,128]{1,0:T(8,128)S(1)} %convolution_bitcast_fusion.2), channel_id=1, replica_groups=mesh['chain'=8,'col'=4] {'col'}, use_global_device_ids=true, to_apply=%region_6.6 | all-reduce | flops 4096 | bytes 32768 | tf_op jit(solution)/shard_map/while/body/eval_jaxpr/psum | solution.py:48
  39.9 1.5 fusion.84
  41.4 31.1 %all-gather.6 = bf16[256,128]{1,0:T(8,128)(2,1)S(1)} all-gather(bf16[32,128]{1,0:T(8,128)(2,1)S(1)} %fusion.84), channel_id=2, replica_groups=mesh['chain'=8,'col'=4] {'chain'}, dimensions={0}, use_global_device_ids=true | all-gather | bytes 73728 | tf_op jit(solution)/shard_map/while/body/eval_jaxpr/all_gather | solution.py:54
  81.5 1.1 convolution_bitcast_fusion.2
  82.6 10.1 %psum.16 = f32[32,128]{1,0:T(8,128)S(1)} all-reduce(f32[32,128]{1,0:T(8,128)S(1)} %convolution_bitcast_fusion.2), channel_id=1, replica_groups=mesh['chain'=8,'col'=4] {'col'}, use_global_device_ids=true, to_apply=%region_6.6 | all-reduce | flops 4096 | bytes 32768 | tf_op jit(solution)/shard_map/while/body/eval_jaxpr/psum | solution.py:48
  92.8 1.5 fusion.84
  94.2 30.6 %all-gather.6 = bf16[256,128]{1,0:T(8,128)(2,1)S(1)} all-gather(bf16[32,128]{1,0:T(8,128)(2,1)S(1)} %fusion.84), channel_id=2, replica_groups=mesh['chain'=8,'col'=4] {'chain'}, dimensions={0}, use_global_device_ids=true | all-gather | bytes 73728 | tf_op jit(solution)/shard_map/while/body/eval_jaxpr/all_gather | solution.py:54
  133.8 1.1 convolution_bitcast_fusion.2
  135.0 10.1 %psum.16 = f32[32,128]{1,0:T(8,128)S(1)} all-reduce(f32[32,128]{1,0:T(8,128)S(1)} %convolution_bitcast_fusion.2), channel_id=1, replica_groups=mesh['chain'=8,'col'=4] {'col'}, use_global_device_ids=true, to_apply=%region_6.6 | all-reduce | flops 4096 | bytes 32768 | tf_op jit(solution)/shard_map/while/body/eval_jaxpr/psum | solution.py:48
  145.1 1.5 fusion.84
  146.6 30.6 %all-gather.6 = bf16[256,128]{1,0:T(8,128)(2,1)S(1)} all-gather(bf16[32,128]{1,0:T(8,128)(2,1)S(1)} %fusion.84), channel_id=2, replica_groups=mesh['chain'=8,'col'=4] {'chain'}, dimensions={0}, use_global_device_ids=true | all-gather | bytes 73728 | tf_op jit(solution)/shard_map/while/body/eval_jaxpr/all_gather | solution.py:54
  186.2 1.1 convolution_bitcast_fusion.2
  187.3 10.1 %psum.16 = f32[32,128]{1,0:T(8,128)S(1)} all-reduce(f32[32,128]{1,0:T(8,128)S(1)} %convolution_bitcast_fusion.2), channel_id=1, replica_groups=mesh['chain'=8,'col'=4] {'col'}, use_global_device_ids=true, to_apply=%region_6.6 | all-reduce | flops 4096 | bytes 32768 | tf_op jit(solution)/shard_map/while/body/eval_jaxpr/psum | solution.py:48
  197.4 1.5 fusion.84
  198.9 30.6 %all-gather.6 = bf16[256,128]{1,0:T(8,128)(2,1)S(1)} all-gather(bf16[32,128]{1,0:T(8,128)(2,1)S(1)} %fusion.84), channel_id=2, replica_groups=mesh['chain'=8,'col'=4] {'chain'}, dimensions={0}, use_global_device_ids=true | all-gather | bytes 73728 | tf_op jit(solution)/shard_map/while/body/eval_jaxpr/all_gather | solution.py:54
  238.5 1.1 convolution_bitcast_fusion.2
  239.6 10.1 %psum.16 = f32[32,128]{1,0:T(8,128)S(1)} all-reduce(f32[32,128]{1,0:T(8,128)S(1)} %convolution_bitcast_fusion.2), channel_id=1, replica_groups=mesh['chain'=8,'col'=4] {'col'}, use_global_device_ids=true, to_apply=%region_6.6 | all-reduce | flops 4096 | bytes 32768 | tf_op jit(solution)/shard_map/while/body/eval_jaxpr/psum | solution.py:48
  249.8 1.5 fusion.84
  251.2 30.6 %all-gather.6 = bf16[256,128]{1,0:T(8,128)(2,1)S(1)} all-gather(bf16[32,128]{1,0:T(8,128)(2,1)S(1)} %fusion.84), channel_id=2, replica_groups=mesh['chain'=8,'col'=4] {'chain'}, dimensions={0}, use_global_device_ids=true | all-gather | bytes 73728 | tf_op jit(solution)/shard_map/while/body/eval_jaxpr/all_gather | solution.py:54
  290.8 1.1 convolution_bitcast_fusion.2
  291.9 10.1 %psum.16 = f32[32,128]{1,0:T(8,128)S(1)} all-reduce(f32[32,128]{1,0:T(8,128)S(1)} %convolution_bitcast_fusion.2), channel_id=1, replica_groups=mesh['chain'=8,'col'=4] {'col'}, use_global_device_ids=true, to_apply=%region_6.6 | all-reduce | flops 4096 | bytes 32768 | tf_op jit(solution)/shard_map/while/body/eval_jaxpr/psum | solution.py:48
  302.1 1.5 fusion.84
  303.6 30.6 %all-gather.6 = bf16[256,128]{1,0:T(8,128)(2,1)S(1)} all-gather(bf16[32,128]{1,0:T(8,128)(2,1)S(1)} %fusion.84), channel_id=2, replica_groups=mesh['chain'=8,'col'=4] {'chain'}, dimensions={0}, use_global_device_ids=true | all-gather | bytes 73728 | tf_op jit(solution)/shard_map/while/body/eval_jaxpr/all_gather | solution.py:54
  338.2 249.2 %while.36 = (s32[]{:T(128)}, f32[4,32,128]{2,0,1:T(4,128)S(1)}, bf16[4,32,128]{2,1,0:T(8,128)(2,1)S(1)}, s32[24]{0:T(128)S(1)}, s32[24]{0:T(128)S(1)}, /*index=5...) while((s32[]{:T(128)}, f32[4,32,128]{2,0,1:T(4,128)S(1)}, ...), condition=%wide.region_18.19_spmd.clone.clone, body=%wide.region_14.18_spmd.clone.clone.sunk | while | flops 31032652 | bytes 2840456 | solution.py:128
  341.7 5.2 all_gather.28
  347.7 30.5 %all-gather.7 = bf16[256,128]{1,0:T(8,128)(2,1)S(1)} all-gather(bf16[32,128]{1,0:T(8,128)(2,1)S(1)} %fusion.94), channel_id=3, replica_groups=mesh['chain'=8,'col'=4] {'chain'}, dimensions={0}, use_global_device_ids=true | all-gather | bytes 73728 | tf_op jit(solution)/shard_map/while/body/eval_jaxpr/all_gather | solution.py:111
  383.2 5.2 all_gather.28
  388.5 0.8 fusion.94
  389.3 30.5 %all-gather.7 = bf16[256,128]{1,0:T(8,128)(2,1)S(1)} all-gather(bf16[32,128]{1,0:T(8,128)(2,1)S(1)} %fusion.94), channel_id=3, replica_groups=mesh['chain'=8,'col'=4] {'chain'}, dimensions={0}, use_global_device_ids=true | all-gather | bytes 73728 | tf_op jit(solution)/shard_map/while/body/eval_jaxpr/all_gather | solution.py:111
  424.8 5.2 all_gather.28
  430.0 0.8 fusion.94
  430.8 30.5 %all-gather.7 = bf16[256,128]{1,0:T(8,128)(2,1)S(1)} all-gather(bf16[32,128]{1,0:T(8,128)(2,1)S(1)} %fusion.94), channel_id=3, replica_groups=mesh['chain'=8,'col'=4] {'chain'}, dimensions={0}, use_global_device_ids=true | all-gather | bytes 73728 | tf_op jit(solution)/shard_map/while/body/eval_jaxpr/all_gather | solution.py:111
  466.3 5.2 all_gather.28
  471.5 0.8 fusion.94
  472.3 30.5 %all-gather.7 = bf16[256,128]{1,0:T(8,128)(2,1)S(1)} all-gather(bf16[32,128]{1,0:T(8,128)(2,1)S(1)} %fusion.94), channel_id=3, replica_groups=mesh['chain'=8,'col'=4] {'chain'}, dimensions={0}, use_global_device_ids=true | all-gather | bytes 73728 | tf_op jit(solution)/shard_map/while/body/eval_jaxpr/all_gather | solution.py:111
  507.8 5.2 all_gather.28
  513.8 30.5 %all-gather.7 = bf16[256,128]{1,0:T(8,128)(2,1)S(1)} all-gather(bf16[32,128]{1,0:T(8,128)(2,1)S(1)} %fusion.94), channel_id=3, replica_groups=mesh['chain'=8,'col'=4] {'chain'}, dimensions={0}, use_global_device_ids=true | all-gather | bytes 73728 | tf_op jit(solution)/shard_map/while/body/eval_jaxpr/all_gather | solution.py:111
  549.4 5.2 all_gather.28
  555.4 30.5 %all-gather.7 = bf16[256,128]{1,0:T(8,128)(2,1)S(1)} all-gather(bf16[32,128]{1,0:T(8,128)(2,1)S(1)} %fusion.94), channel_id=3, replica_groups=mesh['chain'=8,'col'=4] {'chain'}, dimensions={0}, use_global_device_ids=true | all-gather | bytes 73728 | tf_op jit(solution)/shard_map/while/body/eval_jaxpr/all_gather | solution.py:111
  (187 shorter events, 55.3 us)
Async XLA Ops:
  4.0 13.8 %all-to-all-start = ((s32[8,3,2]{1,2,0:T(2,128)}), s32[8,3,2]{1,2,0:T(2,128)S(1)}, u32[]{:S(2)}, u32[]{:S(2)}) async-start(s32[8,3,2]{1,2,0:T(2,128)} %copy.18), calls=%async_computation | async-start | bytes 16384 | tf_op jit(solution)/shard_map/all_to_all | solution.py:87
  17.8 5.3 copy-start.2
  17.8 320.4 %all-to-all-start.1 = ((bf16[8,3,128,128]{3,2,1,0:T(8,128)(2,1)}), bf16[8,3,128,128]{3,2,1,0:T(8,128)(2,1)S(1)}, u32[]{:S(2)}, u32[]{:S(2)}) async-start(bf16[8,3,128,128]{3,2,1,0:T(8,128)(2,1)} %bitcast.42), calls=%async_computation.1 | async-start | bytes 1572864 | tf_op jit(solution)/shard_map/all_to_all | solution.py:86
  587.4 0.6 copy-start
  587.4 0.6 copy-start.1
